TPU v7x, 256 devices: a whole 4x4x8 slice. The times are simulated.
256 devices in a mesh: row: 8 (over x, core), col: 16 (over z, y_hi), layer: 2 (over y_lo).
Axes of the slice: x: 4, y: 4 (y_hi: 2, y_lo: 2; y = y_hi * 2 + y_lo), z: 8, core: 2. Of those that a mesh axis runs over, the one named last changes fastest.
Arguments:
- interface_panel: float32 [2048, 1024], P('col', 'row'), may hold values from -6 to 6
- coupling: float32 [2, 2, 2048, 2048], P('layer', None, 'row', 'col'), may hold values from -0.0625 to 0.0625
- solved_coupling: float32 [8192, 1024], P(('layer', 'col'), 'row'), may hold values from -6 to 6
Outputs:
- schur_panel: float32 [2048, 1024], P('col', 'row')
All inputs are finite; a program needn't handle non-finite values.
Results may differ from a plain program's by a relative error of at most 0.00007.
Values sent between devices are 32-bit elements; how exact they have to be, the bound alone decides.
A program may use at most 64 MiB of HBM per device.

v0:
```python
import jax
import jax.numpy as jnp
from jax import lax
from jax.sharding import PartitionSpec as P


def shards(interface_panel, coupling, solved_coupling):
    blocks = coupling[0]
    depth = blocks.shape[0] * blocks.shape[1] * lax.axis_size("row")
    gathered_b = lax.all_gather(blocks, "row", axis=1, tiled=True).reshape(depth, blocks.shape[2])
    gathered_y = lax.all_gather(solved_coupling, "col", axis=0, tiled=True)
    partial = lax.dot_general(
        gathered_b,
        gathered_y,
        (((0,), (0,)), ((), ())),
        precision=lax.Precision.HIGHEST,
        preferred_element_type=jnp.float32,
    )
    other = lax.ppermute(partial, "layer", [(0, 1), (1, 0)])
    return interface_panel - (partial + other)


def solution(mesh):
    return jax.shard_map(
        shards,
        mesh=mesh,
        in_specs=(P("col", "row"), P("layer", None, "row", "col"), P(("layer", "col"), "row")),
        out_specs=P("col", "row"),
        check_vma=False,
    )
```

profile of v0, /device:TPU:2, one launch (start us, length us, event | category | flops | bytes accessed | tf_op | source)
XLA Modules:
  0.0 145.9 jit_solution(16994233739036828383)
XLA Ops:
  6.5 0.0 all-gather.6.cloned.1.call-start
  6.5 0.7 all-gather.6.cloned.1.call-update
  7.3 0.0 all-gather.4.cloned.1.call-start
  7.3 0.7 all-gather.4.cloned.1.call-update
  8.0 31.0 %all-gather.6.cloned.1.call-done = f32[1,2,2048,128]{3,2,1,0:T(8,128)} async-done(((f32[1,2,256,128]{3,2,1,0:T(8,128)}), f32[1,2,2048,128]{3,2,1,0:T(8,128)}) %all-gather.6.cloned.1.call-update) | async-done | bytes 2097168 | tf_op jit(solution)/shard_map/all_gather | solution.py:10
  39.0 89.4 %all-gather.4.cloned.1.call-done = f32[4096,128]{1,0:T(8,128)} async-done(((f32[256,128]{1,0:T(8,128)}), f32[4096,128]{1,0:T(8,128)}) %all-gather.4.cloned.1.call-update) | async-done | bytes 2097168 | tf_op jit(solution)/shard_map/all_gather | solution.py:11
  128.4 0.0 copy-start
  128.4 5.7 %fusion = f32[128,128]{1,0:T(8,128)S(1)} fusion(f32[4096,128]{1,0:T(8,128)} %bitcast.3, f32[4096,128]{1,0:T(8,128)} %all-gather.4.cloned.1.call-done), kind=kOutput, calls=%fused_computation.1 | convolution fusion | flops 805306368 | bytes 4259840 | tf_op jit(solution)/shard_map/dot_general | solution.py:12
  134.1 0.7 collective-permute-start
  134.7 3.7 %collective-permute-done = f32[128,128]{1,0:T(8,128)S(1)} collective-permute-done((f32[128,128]{1,0:T(8,128)S(1)}, f32[128,128]{1,0:T(8,128)S(1)}, u32[]{:S(2)}, u32[]{:S(2)}) %collective-permute-start) | collective-permute-done | bytes 65568 | tf_op jit(solution)/shard_map/ppermute | solution.py:19
  138.4 0.0 copy-done
  138.4 0.6 add_subtract_fusion
Async XLA Ops:
  6.5 32.4 %all-gather.6.cloned.1.call-start = ((), (), s32[]{:S(2)}) async-start(), calls=%async_computation.1 | async-start | bytes 2359296 | tf_op jit(solution)/shard_map/all_gather | solution.py:10
  7.3 121.1 %all-gather.4.cloned.1.call-start = ((), (), s32[]{:S(2)}) async-start(), calls=%async_computation | async-start | bytes 2228224 | tf_op jit(solution)/shard_map/all_gather | solution.py:11
  128.4 10.1 %copy-start = (f32[128,128]{1,0:T(8,128)S(1)}, f32[128,128]{1,0:T(8,128)}, u32[]{:S(2)}) copy-start(f32[128,128]{1,0:T(8,128)} %param.3) | copy-start | bytes 196612
  134.1 4.4 %collective-permute-start = (f32[128,128]{1,0:T(8,128)S(1)}, f32[128,128]{1,0:T(8,128)S(1)}, u32[]{:S(2)}, u32[]{:S(2)}) collective-permute-start(f32[128,128]{1,0:T(8,128)S(1)} %fusion), channel_id=1, source_target_pairs={{0,1},{1,0},{2,3},{3,2},{4,5},{5,4},{6,7},{7,6},{8,9},{9,8},{10,11... | collective-permute-start | bytes 196616 | tf_op jit(solution)/shard_map/ppermute | solution.py:19
Sparse Core Ops, SparseCore 0:
  9.2 29.7 all-gather.5
  41.6 86.7 all-gather.3
where the time goes:
time: 146 us
  waiting for transfers between devices  125 us (86%)
  between operations  13.4 us (9%)
  matrix products  5.7 us (4%)
    all_gather x1, waiting for transfers between devices, shards(): gathered_y = lax.all_gather(solved_coupling, 'col', axis=0, tiled=True)  89.4 us
    all_gather x1, waiting for transfers between devices, shards(): lax.all_gather(blocks, 'row', axis=1, tiled=True)  31 us
    dot_general x1, matrix products, shards(): lax.dot_general(gathered_b, gathered_y, (((0,), (0,)), ((), ())), precisi...  5.7 us
    ppermute x1, waiting for transfers between devices, shards(): other = lax.ppermute(partial, 'layer', [(0, 1), (1, 0)])  3.68 us
  transfers between devices with their start and end apart: 3, of which 3 were waited for; matrix products, arithmetic and copies ran while one was open for 0% of the time, Pallas kernels for 0%

commit v1 on v0

--- a/solution.py
+++ b/solution.py
@@ -4,10 +4,18 @@
 from jax.sharding import PartitionSpec as P
 
 
+def tiled_gather(shard, axis, dim):
+    devices = lax.axis_size(axis)
+    repeats = [devices if d == dim else 1 for d in range(shard.ndim)]
+    return lax.all_to_all(
+        jnp.tile(shard, repeats), axis, split_axis=dim, concat_axis=dim, tiled=True
+    )
+
+
 def shards(interface_panel, coupling, solved_coupling):
     blocks = coupling[0]
     depth = blocks.shape[0] * blocks.shape[1] * lax.axis_size("row")
-    gathered_b = lax.all_gather(blocks, "row", axis=1, tiled=True).reshape(depth, blocks.shape[2])
+    gathered_b = tiled_gather(blocks, "row", 1).reshape(depth, blocks.shape[2])
     gathered_y = lax.all_gather(solved_coupling, "col", axis=0, tiled=True)
     partial = lax.dot_general(
         gathered_b,

time: 146 us -> 116 us (0.79)
  waiting for transfers between devices: 125 us -> 63.1 us
  blocking collectives: 0 us -> 30.8 us
  local copies, waits for them, and re-layouts: 0.01 us -> 1.84 us
    all_gather x1 -> x0, waiting for transfers between devices: 31 us -> none  [shards(): lax.all_gather(blocks, 'row', axis=1, tiled=True)]
    all_to_all x0 -> x1, blocking collectives: none -> 30.8 us  [tiled_gather(): lax.all_to_all(jnp.tile(shard, repeats), axis, split_axis=dim, concat_axi...]
    all_gather x1, waiting for transfers between devices: 89.4 us -> 58.7 us  [shards(): gathered_y = lax.all_gather(solved_coupling, 'col', axis=0, tiled=True)]
    another operation x0 -> x2, local copies, waits for them, and re-layouts: none -> 1.7 us  [tiled_gather(): jnp.tile(shard, repeats)]
  transfers between devices with their start and end apart: 3 -> 2, of which waited for: 3 -> 2; matrix products, arithmetic and copies ran while one was open for 0% -> 2% of each run, Pallas kernels for 0% -> 0%
where the time goes in v1:
time: 116 us; the launch traced here: 115 us
  waiting for transfers between devices  63.1 us (54%)
  blocking collectives  30.8 us (27%)
  between operations  13.4 us (12%)
  matrix products  5.07 us (4%)
  local copies, waits for them, and re-layouts  1.84 us (2%)
    all_gather x1, waiting for transfers between devices, shards(): gathered_y = lax.all_gather(solved_coupling, 'col', axis=0, tiled=True)  58.7 us
    all_to_all x1, blocking collectives, tiled_gather(): lax.all_to_all(jnp.tile(shard, repeats), axis, split_axis=dim, concat_axi...  30.8 us
    dot_general x1, matrix products, shards(): lax.dot_general(gathered_b, gathered_y, (((0,), (0,)), ((), ())), precisi...  5.07 us
    ppermute x1, waiting for transfers between devices, shards(): other = lax.ppermute(partial, 'layer', [(0, 1), (1, 0)])  3.69 us
  transfers between devices with their start and end apart: 2, of which 2 were waited for; matrix products, arithmetic and copies ran while one was open for 2% of the time, Pallas kernels for 0%

profile of v1, /device:TPU:2, one launch (start us, length us, event | category | flops | bytes accessed | tf_op | source)
XLA Modules:
  0.0 115.5 jit_solution(3972535100533874765)
XLA Ops:
  6.5 0.0 all-gather.2.cloned.1.call-start
  6.5 0.7 all-gather.2.cloned.1.call-update
  7.3 1.2 %copy.5 = f32[2,256,128]{2,0,1:T(2,128)S(1)} copy(f32[2,256,128]{2,1,0:T(8,128)} %bitcast.7) | data formatting | bytes 524288 | tf_op jit(solution)/shard_map/tile | solution.py:11
  8.4 0.5 tile.11
  9.0 30.8 %all_to_all.5 = f32[2,2048,128]{2,0,1:T(2,128)S(1)} all-to-all(f32[2,2048,128]{2,0,1:T(2,128)S(1)} %bitcast.6), channel_id=1, replica_groups=mesh['row'=8,'col'=16,'layer'=2] {'row'}, dimensions={1} | all-to-all | bytes 4194304 | tf_op jit(solution)/shard_map/all_to_all | solution.py:10
  39.7 0.1 copy.6
  39.9 58.7 %all-gather.2.cloned.1.call-done = f32[4096,128]{1,0:T(8,128)} async-done(((f32[256,128]{1,0:T(8,128)}), f32[4096,128]{1,0:T(8,128)}) %all-gather.2.cloned.1.call-update) | async-done | bytes 2097168 | tf_op jit(solution)/shard_map/all_gather | solution.py:19
  98.5 0.0 copy-start
  98.5 5.1 %fusion = f32[128,128]{1,0:T(8,128)S(1)} fusion(f32[4096,128]{1,0:T(8,128)S(1)} %bitcast.5, f32[4096,128]{1,0:T(8,128)} %all-gather.2.cloned.1.call-done), kind=kOutput, calls=%fused_computation.1 | convolution fusion | flops 805306368 | bytes 4259840 | tf_op jit(solution)/shard_map/dot_general | solution.py:20
  103.6 0.7 collective-permute-start
  104.3 3.7 %collective-permute-done = f32[128,128]{1,0:T(8,128)S(1)} collective-permute-done((f32[128,128]{1,0:T(8,128)S(1)}, f32[128,128]{1,0:T(8,128)S(1)}, u32[]{:S(2)}, u32[]{:S(2)}) %collective-permute-start) | collective-permute-done | bytes 65568 | tf_op jit(solution)/shard_map/ppermute | solution.py:27
  108.0 0.0 copy-done
  108.0 0.6 add_subtract_fusion
Async XLA Ops:
  6.5 92.0 %all-gather.2.cloned.1.call-start = ((), (), s32[]{:S(2)}) async-start(), calls=%async_computation.1 | async-start | bytes 2228224 | tf_op jit(solution)/shard_map/all_gather | solution.py:19
  98.5 9.4 %copy-start = (f32[128,128]{1,0:T(8,128)S(1)}, f32[128,128]{1,0:T(8,128)}, u32[]{:S(2)}) copy-start(f32[128,128]{1,0:T(8,128)} %param.3) | copy-start | bytes 196612
  103.6 4.4 %collective-permute-start = (f32[128,128]{1,0:T(8,128)S(1)}, f32[128,128]{1,0:T(8,128)S(1)}, u32[]{:S(2)}, u32[]{:S(2)}) collective-permute-start(f32[128,128]{1,0:T(8,128)S(1)} %fusion), channel_id=1, source_target_pairs={{0,1},{1,0},{2,3},{3,2},{4,5},{5,4},{6,7},{7,6},{8,9},{9,8},{10,11... | collective-permute-start | bytes 196616 | tf_op jit(solution)/shard_map/ppermute | solution.py:27
Sparse Core Ops, SparseCore 0:
  9.9 88.5 all-gather.1
